TPU v7x, 32 devices: a whole 2x2x4 slice. The times are simulated.
32 devices in a mesh: grp: 8 (over z, core), sp: 4 (over y, x).
Axes of the slice: x: 2, y: 2, z: 4, core: 2. Of those that a mesh axis runs over, the one named last changes fastest.
Arguments:
- acts: bfloat16 [32, 4, 16, 728], P('grp', 'sp'), may hold values from -6 to 6
- cotangent: bfloat16 [32, 4, 16, 728], P(('grp', 'sp')), may hold values from -6 to 6
- depth_kernel: float32 [3, 3, 728], replicated, may hold values from -2 to 2
- point_weight: bfloat16 [728, 728], replicated, may hold values from -0.21875 to 0.21875
- batch_norm_gain: float32 [728], replicated, may hold values from 0.5 to 2
- norm_shift_bias: float32 [728], replicated, may hold values from -1 to 1
Outputs:
- block_out: bfloat16 [32, 4, 16, 728], P(('grp', 'sp'))
- input_grad: bfloat16 [32, 4, 16, 728], P('grp', 'sp')
- weight_grad: float32 [529984], P('sp')
All inputs are finite; a program needn't handle non-finite values.
Results may differ from a plain program's by a relative error of at most 0.018.
Values may be sent and summed in bfloat16 or wider, within the bound.
A program may use at most 64 MiB of HBM per device.

v0:
```python
import jax
import jax.numpy as jnp
from jax import lax
from jax.sharding import PartitionSpec as P


def depth_forward(field, filter_weight):
    rows = field.shape[1]
    cols = field.shape[2]
    padded = jnp.pad(field, ((0, 0), (1, 1), (1, 1), (0, 0)))
    total = jnp.zeros(field.shape, jnp.float32)
    for i in range(3):
        for j in range(3):
            total = total + padded[:, i : i + rows, j : j + cols, :] * filter_weight[i, j]
    return total


def depth_backward(field, filter_weight):
    rows = field.shape[1]
    cols = field.shape[2]
    padded = jnp.pad(field, ((0, 0), (1, 1), (1, 1), (0, 0)))
    total = jnp.zeros(field.shape, jnp.float32)
    for i in range(3):
        for j in range(3):
            total = (
                total
                + padded[:, 2 - i : 2 - i + rows, 2 - j : 2 - j + cols, :] * filter_weight[i, j]
            )
    return total


def body(acts, cotangent, depth_kernel, point_weight, batch_norm_gain, norm_shift_bias):
    channel_count = acts.shape[-1]
    sample_image = lax.all_to_all(acts, "sp", split_axis=0, concat_axis=1, tiled=True)
    input_single_precision = sample_image.astype(jnp.float32)
    hidden = jnp.maximum(input_single_precision, 0.0)
    depthed = depth_forward(hidden, depth_kernel).astype(jnp.bfloat16)
    flat_d = depthed.reshape(-1, channel_count)
    element_count = flat_d.shape[0] * lax.axis_size("sp")
    projected_output = jnp.dot(flat_d, point_weight, preferred_element_type=jnp.float32)
    total, squares = lax.psum(
        (jnp.sum(projected_output, axis=0), jnp.sum(projected_output * projected_output, axis=0)),
        "sp",
    )
    batch_mean = total / element_count
    var = squares / element_count - batch_mean * batch_mean
    inverse_deviation = lax.rsqrt(var + 1e-05)
    normalized_input = (projected_output - batch_mean) * inverse_deviation
    block_out = (
        (
            input_single_precision.reshape(-1, channel_count)
            + batch_norm_gain * normalized_input
            + norm_shift_bias
        )
        .astype(jnp.bfloat16)
        .reshape(sample_image.shape)
    )
    gfloat = cotangent.astype(jnp.float32).reshape(-1, channel_count)
    scaled_output = gfloat * batch_norm_gain
    leading_layer, second_layer = lax.psum(
        (jnp.sum(scaled_output, axis=0), jnp.sum(scaled_output * normalized_input, axis=0)), "sp"
    )
    projected_gradient = (
        inverse_deviation
        * (
            scaled_output
            - leading_layer / element_count
            - normalized_input * (second_layer / element_count)
        )
    ).astype(jnp.bfloat16)
    local_weight = jnp.dot(
        flat_d.T, projected_gradient, preferred_element_type=jnp.float32
    ).reshape(-1)
    ddepth = jnp.dot(
        projected_gradient, point_weight.T, preferred_element_type=jnp.float32
    ).reshape(sample_image.shape)
    dhidden = depth_backward(ddepth, depth_kernel)
    dinput = (
        gfloat.reshape(sample_image.shape) + jnp.where(sample_image > 0, dhidden, 0.0)
    ).astype(jnp.bfloat16)
    input_grad = lax.all_to_all(dinput, "sp", split_axis=1, concat_axis=0, tiled=True)
    slices = lax.psum_scatter(
        local_weight.astype(jnp.bfloat16), "sp", scatter_dimension=0, tiled=True
    ).astype(jnp.float32)
    weight_grad = lax.psum(slices, "grp")
    return (block_out, input_grad, weight_grad)


def solution(mesh):
    in_specs = (P("grp", "sp", None, None), P(("grp", "sp"), None, None, None), P(), P(), P(), P())
    out_specs = (P(("grp", "sp"), None, None, None), P("grp", "sp", None, None), P("sp"))
    return jax.shard_map(body, mesh=mesh, in_specs=in_specs, out_specs=out_specs, check_vma=False)
```

profile of v0, /device:TPU:0, one launch (start us, length us, event | category | flops | bytes accessed | tf_op | source)
XLA Modules:
  0.0 160.6 jit_solution(10437990497592473162)
XLA Ops:
  7.2 5.3 %all-to-all-start = ((bf16[4,1,16,728]{3,2,1,0:T(8,128)(2,1)}), bf16[4,1,16,728]{3,2,1,0:T(8,128)(2,1)S(1)}, u32[]{:S(2)}, u32[]{:S(2)}) async-start(bf16[4,1,16,728]{3,2,1,0:T(8,128)(2,1)} %param.6), calls=%async_computation | async-start | bytes 196608 | tf_op jit(solution)/shard_map/all_to_all | solution.py:34
  12.5 0.0 all-reduce.10.cloned.1.call-start
  12.6 1.0 multiply_reduce_fusion.1
  13.5 1.0 slice_reduce_fusion.8
  14.5 3.0 %all-to-all-done = bf16[4,1,16,728]{3,2,1,0:T(8,128)(2,1)S(1)} async-done(((bf16[4,1,16,728]{3,2,1,0:T(8,128)(2,1)}), bf16[4,1,16,728]{3,2,1,0:T(8,128)(2,1)S(1)}, u32[]{:S(2)}, u32[]{:S(2)}) %all-to-all-start) | async-done | bytes 93216 | tf_op jit(solution)/shard_map/all_to_all | solution.py:34
  17.5 0.1 fusion.9
  17.6 0.3 fusion.39
  18.0 8.4 %all-reduce.4 = (f32[728]{0:T(1024)S(1)}, f32[728]{0:T(1024)S(1)}) all-reduce(f32[728]{0:T(1024)S(1)} %get-tuple-element.7, f32[728]{0:T(1024)S(1)} %get-tuple-element.6), channel_id=1, replica_groups=mesh['grp'=8,'sp'=4] {'sp'}, use_global_device_ids=true, to_apply=%region_3.4 | all-reduce | flops 1456 | bytes 11648 | tf_op jit(solution)/shard_map/psum | solution.py:41
  26.5 0.1 multiply_reduce_fusion
  26.5 9.0 %all-reduce.3 = (f32[728]{0:T(1024)S(1)}, f32[728]{0:T(1024)S(1)}) all-reduce(f32[728]{0:T(1024)S(1)} %multiply_reduce_fusion, f32[728]{0:T(1024)S(1)} %multiply_reduce_fusion.1), channel_id=1, replica_groups=mesh['grp'=8,'sp'=4] {'sp'}, use_global_device_ids=true, to_apply=%region_7.8 | all-reduce | flops 1456 | bytes 11648 | tf_op jit(solution)/shard_map/psum | solution.py:60
  35.6 0.7 multiply_convert_fusion
  36.3 0.5 convolution_convert_fusion
  36.8 3.5 %convert_element_type.59 = bf16[529984]{0:T(1024)(128)(2,1)} reshape(bf16[728,728]{1,0:T(8,128)(2,1)S(1)} %convolution_convert_fusion) | data formatting | bytes 2119936 | tf_op jit(solution)/shard_map/convert_element_type | solution.py:83
  40.3 0.0 all-reduce.10.cloned.1.call-update
  40.3 0.0 all-reduce.8.cloned.1.call-start
  40.3 0.6 dynamic-slice
  41.6 0.5 fusion.40
  42.1 51.5 %all-reduce.10.cloned.1.call-done = bf16[529984]{0:T(1024)(128)(2,1)} async-done(((bf16[529984]{0:T(1024)(128)(2,1)}), bf16[529984]{0:T(1024)(128)(2,1)}) %all-reduce.10.cloned.1.call-update) | async-done | bytes 1059984
  93.5 1.9 %dynamic-slice_convert_fusion = f32[132496]{0:T(1024)} fusion(bf16[529984]{0:T(1024)(128)(2,1)} %all-reduce.10.cloned.1.call-done, u32[]{:T(128)S(6)} %multiply.5), kind=kLoop, calls=%fused_computation.17 | loop fusion | flops 132496 | bytes 794980 | tf_op jit(solution)/shard_map/convert_element_type | solution.py:84
  95.5 0.2 fusion.38
  95.7 7.7 %all_to_all.21 = bf16[1,4,16,728]{3,2,0,1:T(8,128)(2,1)S(1)} all-to-all(bf16[1,4,16,728]{3,2,0,1:T(8,128)(2,1)S(1)} %fusion.38), channel_id=1, replica_groups=mesh['grp'=8,'sp'=4] {'sp'}, dimensions={1} | all-to-all | bytes 186368 | tf_op jit(solution)/shard_map/all_to_all | solution.py:81
  103.4 47.9 %all-reduce.8.cloned.1.call-done = f32[132496]{0:T(1024)} async-done(((f32[132496]{0:T(1024)}), f32[132496]{0:T(1024)}) %all-reduce.8.cloned.1.call-update) | async-done | bytes 530000 | tf_op jit(solution)/shard_map/psum | solution.py:85
  151.3 0.6 copy.16
  151.9 1.9 %copy.17 = f32[132496]{0:T(1024)} copy(f32[132496]{0:T(1024)} %all-reduce.8.cloned.1.call-done) | data formatting | bytes 1059968
  (15 shorter events, 0.1 us)
Async XLA Ops:
  7.2 10.5 %copy-start = (bf16[728,728]{1,0:T(8,128)(2,1)S(1)}, bf16[728,728]{1,0:T(8,128)(2,1)}, u32[]{:S(2)}) copy-start(bf16[728,728]{1,0:T(8,128)(2,1)} %param.9) | copy-start | bytes 3179908
  7.2 10.3 %all-to-all-start = ((bf16[4,1,16,728]{3,2,1,0:T(8,128)(2,1)}), bf16[4,1,16,728]{3,2,1,0:T(8,128)(2,1)S(1)}, u32[]{:S(2)}, u32[]{:S(2)}) async-start(bf16[4,1,16,728]{3,2,1,0:T(8,128)(2,1)} %param.6), calls=%async_computation | async-start | bytes 196608 | tf_op jit(solution)/shard_map/all_to_all | solution.py:34
  12.5 13.9 %copy-start.1 = (bf16[1,4,16,728]{3,2,1,0:T(8,128)(2,1)S(1)}, bf16[1,4,16,728]{3,2,1,0:T(8,128)(2,1)}, u32[]{:S(2)}) copy-start(bf16[1,4,16,728]{3,2,1,0:T(8,128)(2,1)} %param.7) | copy-start | bytes 279556
  12.5 13.9 %copy-start.2 = (f32[728]{0:T(1024)S(1)}, f32[728]{0:T(1024)}, u32[]{:S(2)}) copy-start(f32[728]{0:T(1024)} %param.10) | copy-start | bytes 8740
  12.5 81.0 %all-reduce.10.cloned.1.call-start = ((), (), s32[]{:S(2)}) async-start(), calls=%async_computation.3 | async-start | bytes 2121728
  17.6 18.0 %copy-start.3 = (f32[728]{0:T(1024)S(1)}, f32[728]{0:T(1024)}, u32[]{:S(2)}) copy-start(f32[728]{0:T(1024)} %param.11) | copy-start | bytes 8740
  36.8 3.5 %copy-start.4 = (u32[32]{0:T(128)S(1)}, u32[32]{0:T(128)}, u32[]{:S(2)}) copy-start(u32[32]{0:T(128)} %constant.23) | copy-start | bytes 388
  40.3 111.0 %all-reduce.8.cloned.1.call-start = ((), (), s32[]{:S(2)}) async-start(), calls=%async_computation.2 | async-start | bytes 1064960 | tf_op jit(solution)/shard_map/psum | solution.py:85
Sparse Core Ops, SparseCore 0:
  40.4 53.0 all-reduce.9
  96.5 54.7 all-reduce.7
where the time goes:
time: 161 us
  waiting for transfers between devices  102 us (63%)
  blocking collectives  25.1 us (16%)
  between operations  14.8 us (9%)
  local copies, waits for them, and re-layouts  7.53 us (5%)
  starting transfers between devices  5.41 us (3%)
  other arithmetic  4.04 us (3%)
    unnamed x3, waiting for transfers between devices  51.5 us
    psum x1, waiting for transfers between devices, body(): weight_grad = lax.psum(slices, 'grp')  47.9 us
    psum x1, blocking collectives, body(): lax.psum((jnp.sum(scaled_output, axis=0), jnp.sum(scaled_output * normali...  8.99 us
    psum x1, blocking collectives, body(): lax.psum((jnp.sum(projected_output, axis=0), jnp.sum(projected_output * p...  8.45 us
    all_to_all x1, blocking collectives, body(): lax.all_to_all(dinput, 'sp', split_axis=1, concat_axis=0, tiled=True)  7.68 us
    all_to_all x1, starting transfers between devices, body(): lax.all_to_all(acts, 'sp', split_axis=0, concat_axis=1, tiled=True)  5.34 us
    convert_element_type x1, local copies, waits for them, and re-layouts, body(): local_weight.astype(jnp.bfloat16)  3.46 us
  transfers between devices with their start and end apart: 3, of which 3 were waited for; matrix products, arithmetic and copies ran while one was open for 2% of the time, Pallas kernels for 0%

commit v1 on v0

--- a/solution.py
+++ b/solution.py
@@ -82,7 +82,11 @@
     slices = lax.psum_scatter(
         local_weight.astype(jnp.bfloat16), "sp", scatter_dimension=0, tiled=True
     ).astype(jnp.float32)
-    weight_grad = lax.psum(slices, "grp")
+    weight_grad = slices
+    for hop in (1, 2, 4):
+        weight_grad = weight_grad + lax.ppermute(
+            weight_grad, "grp", [(dev, dev ^ hop) for dev in range(8)]
+        )
     return (block_out, input_grad, weight_grad)
 
 

time: 161 us -> 147 us (0.913)
  waiting for transfers between devices: 102 us -> 84.4 us
  starting transfers between devices: 5.41 us -> 9.46 us
  local copies, waits for them, and re-layouts: 7.53 us -> 5.66 us
    psum x1 -> x0, waiting for transfers between devices: 47.9 us -> none  [body(): weight_grad = lax.psum(slices, 'grp')]
    ppermute x0 -> x3, waiting for transfers between devices: none -> 29.4 us  [body(): lax.ppermute(weight_grad, 'grp', [(dev, dev ^ hop) for dev in range(8)])]
    ppermute x0 -> x3, starting transfers between devices: none -> 4.09 us  [body(): lax.ppermute(weight_grad, 'grp', [(dev, dev ^ hop) for dev in range(8)])]
    add x0 -> x3, other arithmetic: none -> 2.07 us  [body(): weight_grad + lax.ppermute(weight_grad, 'grp', [(dev, dev ^ hop) for dev...]
    unnamed x13 -> x12, local copies, waits for them, and re-layouts: 3.13 us -> 1.25 us
    unnamed x3 -> x2, waiting for transfers between devices: 51.5 us -> 52 us
  transfers between devices with their start and end apart: 3 -> 5, of which waited for: 3 -> 5; matrix products, arithmetic and copies ran while one was open for 2% -> 2% of each run, Pallas kernels for 0% -> 0%
where the time goes in v1:
time: 147 us; the launch traced here: 146 us
  waiting for transfers between devices  84.4 us (57%)
  blocking collectives  25.1 us (17%)
  between operations  14.8 us (10%)
  starting transfers between devices  9.46 us (6%)
  local copies, waits for them, and re-layouts  5.66 us (4%)
  other arithmetic  5.31 us (4%)
    unnamed x2, waiting for transfers between devices  52 us
    ppermute x3, waiting for transfers between devices, body(): lax.ppermute(weight_grad, 'grp', [(dev, dev ^ hop) for dev in range(8)])  29.4 us
    psum x1, blocking collectives, body(): lax.psum((jnp.sum(scaled_output, axis=0), jnp.sum(scaled_output * normali...  8.99 us
    psum x1, blocking collectives, body(): lax.psum((jnp.sum(projected_output, axis=0), jnp.sum(projected_output * p...  8.45 us
    all_to_all x1, blocking collectives, body(): lax.all_to_all(dinput, 'sp', split_axis=1, concat_axis=0, tiled=True)  7.68 us
    all_to_all x1, starting transfers between devices, body(): lax.all_to_all(acts, 'sp', split_axis=0, concat_axis=1, tiled=True)  5.34 us
    ppermute x3, starting transfers between devices, body(): lax.ppermute(weight_grad, 'grp', [(dev, dev ^ hop) for dev in range(8)])  4.09 us
    convert_element_type x1, local copies, waits for them, and re-layouts, body(): local_weight.astype(jnp.bfloat16)  3.46 us
  transfers between devices with their start and end apart: 5, of which 5 were waited for; matrix products, arithmetic and copies ran while one was open for 2% of the time, Pallas kernels for 0%

profile of v1, /device:TPU:0, one launch (start us, length us, event | category | flops | bytes accessed | tf_op | source)
XLA Modules:
  0.0 146.1 jit_solution(13561468147204999503)
XLA Ops:
  7.2 5.3 %all-to-all-start = ((bf16[4,1,16,728]{3,2,1,0:T(8,128)(2,1)}), bf16[4,1,16,728]{3,2,1,0:T(8,128)(2,1)S(1)}, u32[]{:S(2)}, u32[]{:S(2)}) async-start(bf16[4,1,16,728]{3,2,1,0:T(8,128)(2,1)} %param.6), calls=%async_computation | async-start | bytes 196608 | tf_op jit(solution)/shard_map/all_to_all | solution.py:34
  12.6 1.0 multiply_reduce_fusion.1
  13.5 1.0 slice_reduce_fusion.8
  14.5 3.0 %all-to-all-done = bf16[4,1,16,728]{3,2,1,0:T(8,128)(2,1)S(1)} async-done(((bf16[4,1,16,728]{3,2,1,0:T(8,128)(2,1)}), bf16[4,1,16,728]{3,2,1,0:T(8,128)(2,1)S(1)}, u32[]{:S(2)}, u32[]{:S(2)}) %all-to-all-start) | async-done | bytes 93216 | tf_op jit(solution)/shard_map/all_to_all | solution.py:34
  17.6 0.3 fusion.40
  18.0 8.4 %all-reduce.4 = (f32[728]{0:T(1024)S(1)}, f32[728]{0:T(1024)S(1)}) all-reduce(f32[728]{0:T(1024)S(1)} %get-tuple-element.7, f32[728]{0:T(1024)S(1)} %get-tuple-element.6), channel_id=1, replica_groups=mesh['grp'=8,'sp'=4] {'sp'}, use_global_device_ids=true, to_apply=%region_3.4 | all-reduce | flops 1456 | bytes 11648 | tf_op jit(solution)/shard_map/psum | solution.py:41
  26.5 9.0 %all-reduce.3 = (f32[728]{0:T(1024)S(1)}, f32[728]{0:T(1024)S(1)}) all-reduce(f32[728]{0:T(1024)S(1)} %multiply_reduce_fusion, f32[728]{0:T(1024)S(1)} %multiply_reduce_fusion.1), channel_id=1, replica_groups=mesh['grp'=8,'sp'=4] {'sp'}, use_global_device_ids=true, to_apply=%region_7.8 | all-reduce | flops 1456 | bytes 11648 | tf_op jit(solution)/shard_map/psum | solution.py:60
  35.6 0.7 multiply_convert_fusion
  36.3 0.5 convolution_convert_fusion
  36.8 3.5 %convert_element_type.59 = bf16[529984]{0:T(1024)(128)(2,1)} reshape(bf16[728,728]{1,0:T(8,128)(2,1)S(1)} %convolution_convert_fusion) | data formatting | bytes 2119936 | tf_op jit(solution)/shard_map/convert_element_type | solution.py:83
  40.3 0.6 dynamic-slice
  41.5 52.0 %all-reduce.7.cloned.1.call-done = bf16[529984]{0:T(1024)(128)(2,1)} async-done(((bf16[529984]{0:T(1024)(128)(2,1)}), bf16[529984]{0:T(1024)(128)(2,1)}) %all-reduce.7.cloned.1.call-update) | async-done | bytes 1059984
  93.5 1.1 dynamic-slice_convert_fusion
  94.8 1.9 %collective-permute-done = f32[132496]{0:T(1024)S(1)} collective-permute-done((f32[132496]{0:T(1024)S(1)}, f32[132496]{0:T(1024)S(1)}, u32[]{:S(2)}, u32[]{:S(2)}) %collective-permute-start) | collective-permute-done | bytes 530016 | tf_op jit(solution)/shard_map/ppermute | solution.py:87
  96.7 1.1 fusion.38
  97.8 1.6 %collective-permute-start.1 = (f32[132496]{0:T(1024)S(1)}, f32[132496]{0:T(1024)S(1)}, u32[]{:S(2)}, u32[]{:S(2)}) collective-permute-start(f32[132496]{0:T(1024)S(1)} %fusion.38), channel_id=1, source_target_pairs={{0,8},{4,12},{8,0},{12,4},{16,24},{20,28},{24,16},{28,20},{1,9},{5... | collective-permute-start | bytes 1589960 | tf_op jit(solution)/shard_map/ppermute | solution.py:87
  99.3 12.7 %collective-permute-done.1 = f32[132496]{0:T(1024)S(1)} collective-permute-done((f32[132496]{0:T(1024)S(1)}, f32[132496]{0:T(1024)S(1)}, u32[]{:S(2)}, u32[]{:S(2)}) %collective-permute-start.1) | collective-permute-done | bytes 530016 | tf_op jit(solution)/shard_map/ppermute | solution.py:87
  112.1 2.5 %collective-permute-start.2 = (f32[132496]{0:T(1024)S(1)}, f32[132496]{0:T(1024)S(1)}, u32[]{:S(2)}, u32[]{:S(2)}) collective-permute-start(f32[132496]{0:T(1024)S(1)} %add.114), channel_id=1, source_target_pairs={{0,16},{4,20},{8,24},{12,28},{16,0},{20,4},{24,8},{28,12},{1,17},{... | collective-permute-start | bytes 1589960 | tf_op jit(solution)/shard_map/ppermute | solution.py:87
  114.5 0.5 fusion.41
  115.0 0.2 fusion.39
  115.2 7.7 %all_to_all.21 = bf16[1,4,16,728]{3,2,0,1:T(8,128)(2,1)S(1)} all-to-all(bf16[1,4,16,728]{3,2,0,1:T(8,128)(2,1)S(1)} %fusion.39), channel_id=1, replica_groups=mesh['grp'=8,'sp'=4] {'sp'}, dimensions={1} | all-to-all | bytes 186368 | tf_op jit(solution)/shard_map/all_to_all | solution.py:81
  122.9 14.9 %collective-permute-done.2 = f32[132496]{0:T(1024)S(1)} collective-permute-done((f32[132496]{0:T(1024)S(1)}, f32[132496]{0:T(1024)S(1)}, u32[]{:S(2)}, u32[]{:S(2)}) %collective-permute-start.2) | collective-permute-done | bytes 530016 | tf_op jit(solution)/shard_map/ppermute | solution.py:87
  137.7 0.9 add.115
  138.6 0.6 copy.15
  (20 shorter events, 0.5 us)
Async XLA Ops:
  7.2 10.5 %copy-start = (bf16[728,728]{1,0:T(8,128)(2,1)S(1)}, bf16[728,728]{1,0:T(8,128)(2,1)}, u32[]{:S(2)}) copy-start(bf16[728,728]{1,0:T(8,128)(2,1)} %param.9) | copy-start | bytes 3179908
  7.2 10.3 %all-to-all-start = ((bf16[4,1,16,728]{3,2,1,0:T(8,128)(2,1)}), bf16[4,1,16,728]{3,2,1,0:T(8,128)(2,1)S(1)}, u32[]{:S(2)}, u32[]{:S(2)}) async-start(bf16[4,1,16,728]{3,2,1,0:T(8,128)(2,1)} %param.6), calls=%async_computation | async-start | bytes 196608 | tf_op jit(solution)/shard_map/all_to_all | solution.py:34
  12.5 13.9 %copy-start.1 = (bf16[1,4,16,728]{3,2,1,0:T(8,128)(2,1)S(1)}, bf16[1,4,16,728]{3,2,1,0:T(8,128)(2,1)}, u32[]{:S(2)}) copy-start(bf16[1,4,16,728]{3,2,1,0:T(8,128)(2,1)} %param.7) | copy-start | bytes 279556
  12.5 13.9 %copy-start.2 = (f32[728]{0:T(1024)S(1)}, f32[728]{0:T(1024)}, u32[]{:S(2)}) copy-start(f32[728]{0:T(1024)} %param.10) | copy-start | bytes 8740
  12.5 81.0 %all-reduce.7.cloned.1.call-start = ((), (), s32[]{:S(2)}) async-start(), calls=%async_computation.2 | async-start | bytes 2121728
  17.6 18.0 %copy-start.3 = (f32[728]{0:T(1024)S(1)}, f32[728]{0:T(1024)}, u32[]{:S(2)}) copy-start(f32[728]{0:T(1024)} %param.11) | copy-start | bytes 8740
  36.8 3.5 %copy-start.4 = (u32[32]{0:T(128)S(1)}, u32[32]{0:T(128)}, u32[]{:S(2)}) copy-start(u32[32]{0:T(128)} %constant.23) | copy-start | bytes 388
  94.7 2.0 %collective-permute-start = (f32[132496]{0:T(1024)S(1)}, f32[132496]{0:T(1024)S(1)}, u32[]{:S(2)}, u32[]{:S(2)}) collective-permute-start(f32[132496]{0:T(1024)S(1)} %dynamic-slice_convert_fusion), channel_id=1, source_target_pairs={{0,4},{4,0},{8,12},{12,8},{16,20},{20,16},{24,28},{28,24},{1,5},{5... | collective-permute-start | bytes 1589960 | tf_op jit(solution)/shard_map/ppermute | solution.py:87
  97.8 14.2 %collective-permute-start.1 = (f32[132496]{0:T(1024)S(1)}, f32[132496]{0:T(1024)S(1)}, u32[]{:S(2)}, u32[]{:S(2)}) collective-permute-start(f32[132496]{0:T(1024)S(1)} %fusion.38), channel_id=1, source_target_pairs={{0,8},{4,12},{8,0},{12,4},{16,24},{20,28},{24,16},{28,20},{1,9},{5... | collective-permute-start | bytes 1589960 | tf_op jit(solution)/shard_map/ppermute | solution.py:87
  112.1 25.7 %collective-permute-start.2 = (f32[132496]{0:T(1024)S(1)}, f32[132496]{0:T(1024)S(1)}, u32[]{:S(2)}, u32[]{:S(2)}) collective-permute-start(f32[132496]{0:T(1024)S(1)} %add.114), channel_id=1, source_target_pairs={{0,16},{4,20},{8,24},{12,28},{16,0},{20,4},{24,8},{28,12},{1,17},{... | collective-permute-start | bytes 1589960 | tf_op jit(solution)/shard_map/ppermute | solution.py:87
Sparse Core Ops, SparseCore 0:
  40.4 53.0 all-reduce.6
